TPU v7x, 256 devices: a whole 4x4x8 slice. The times are simulated.
256 devices in a mesh: op: 8 (over x, core), sec: 32 (over y, z).
Axes of the slice: x: 4, y: 4, z: 8, core: 2. Of those that a mesh axis runs over, the one named last changes fastest.
Arguments:
- wavefunction: bfloat16 [8192, 3, 4096], P('sec'), may hold values from -6 to 6
- left_ops: bfloat16 [8192, 24, 256], P('sec', 'op'), may hold values from -0.375 to 0.375
- right_ops: bfloat16 [24, 32, 128, 128], P('op', 'sec'), may hold values from -0.109375 to 0.109375
- term_shift: int32 [24], P('op'), may hold values from -1 to 1
Outputs:
- applied: bfloat16 [8192, 3, 4096], P('sec', None, 'op')
All inputs are finite; a program needn't handle non-finite values.
Results may differ from a plain program's by a relative error of at most 0.017.
Values may be sent and summed in bfloat16 or wider, within the bound.
A program may use at most 128 MiB of HBM per device.

v0:
```python
import jax
import jax.numpy as jnp
from jax import lax
from jax.sharding import PartitionSpec as P

ML = 256
MR = 128
VECS = 3


def extended(block, sides, width):
    for axis, dim in sides:
        count = lax.axis_size(axis)
        forward = [(i, i + 1) for i in range(count - 1)]
        backward = [(target, source) for source, target in forward]
        low = lax.ppermute(
            lax.slice_in_dim(block, block.shape[dim] - width, None, axis=dim), axis, forward
        )
        high = lax.ppermute(lax.slice_in_dim(block, 0, width, axis=dim), axis, backward)
        block = jnp.concatenate([low, block, high], axis=dim)
    return block


def on_device(wavefunction, left_ops, right_ops, term_shift):
    columns = wavefunction.shape[2]
    right_count = columns // MR
    term_count = left_ops.shape[1]
    packed = jnp.concatenate(
        [wavefunction.reshape(ML, VECS * columns), left_ops.reshape(ML, term_count * ML)], axis=1
    )
    padded = extended(packed, (("sec", 0),), ML)
    right_all = lax.all_gather(right_ops, "sec", axis=1, tiled=True)
    every_col = jnp.arange(right_count)
    total = jnp.zeros((ML, VECS, columns), jnp.float32)
    for inner in range(term_count):
        offset = term_shift[inner]
        rows_block = lax.dynamic_slice_in_dim(padded, (1 - offset) * ML, ML, 0)
        source = rows_block[:, : VECS * columns].reshape(ML, VECS, columns)
        left_block = rows_block[:, VECS * columns + inner * ML : VECS * columns + (inner + 1) * ML]
        product = jnp.einsum(
            "ij,jvn->ivn", left_block, source, preferred_element_type=jnp.float32
        ).astype(jnp.bfloat16)
        rolled = jnp.roll(product, -offset * MR, axis=2).reshape(ML, VECS, right_count, MR)
        result = jnp.einsum(
            "ivrk,rkm->ivrm", rolled, right_all[inner], preferred_element_type=jnp.float32
        )
        col_valid = (every_col + offset >= 0) & (every_col + offset < right_count)
        result = jnp.where(col_valid[None, None, :, None], result, jnp.zeros((), jnp.float32))
        total = total + result.reshape(ML, VECS, columns)
    row_layout = total.astype(jnp.bfloat16)
    summed = lax.psum_scatter(
        row_layout.astype(jnp.float32).astype(jnp.bfloat16), "op", scatter_dimension=2, tiled=True
    )
    return summed


def solution(mesh):
    in_specs = (P("sec", None, None), P("sec", "op", None), P("op", "sec", None, None), P("op"))
    out_specs = P("sec", None, "op")
    return jax.shard_map(
        on_device, mesh=mesh, in_specs=in_specs, out_specs=out_specs, check_vma=False
    )
```

profile of v0, /device:TPU:16, one launch (start us, length us, event | category | flops | bytes accessed | tf_op | source)
XLA Modules:
  0.0 404.6 jit_solution(8244802303366302837)
XLA Ops:
  7.9 8.6 %copy.10 = bf16[256,3,4096]{0,2,1:T(8,128)(2,1)} copy(bf16[256,3,4096]{2,0,1:T(8,128)(2,1)} %param.6) | data formatting | bytes 12582912 | tf_op args[0]
  16.5 8.6 %copy.12 = bf16[256,12288]{1,0:T(8,128)(2,1)} copy(bf16[256,12288]{0,1:T(8,128)(2,1)} %bitcast.53) | data formatting | bytes 12582912 | tf_op jit(solution)/shard_map/reshape | solution.py:29
  25.2 6.1 %pad_maximum_fusion.1 = bf16[256,13056]{1,0:T(8,128)(2,1)} fusion(bf16[256,768]{1,0:T(8,128)(2,1)S(1)} %copy.13, bf16[256,12288]{1,0:T(8,128)(2,1)} %copy.12), kind=kLoop, calls=%fused_computation.11 | loop fusion | flops 13369344 | bytes 13369344 | tf_op jit(solution)/shard_map/concatenate | solution.py:28
  31.3 7.6 %collective-permute-start.1 = (bf16[256,13056]{1,0:T(8,128)(2,1)}, bf16[256,13056]{1,0:T(8,128)(2,1)}, u32[]{:S(2)}, u32[]{:S(2)}) collective-permute-start(bf16[256,13056]{1,0:T(8,128)(2,1)} %pad_maximum_fusion.1), channel_id=1, source_target_pairs={{1,0},{2,1},{3,2},{4,3},{5,4},{6,5},{7,6},{8,7},{9,8},{10,9},{11,1... | collective-permute-start | bytes 20054024 | tf_op jit(solution)/shard_map/ppermute | solution.py:19
  47.8 153.0 %collective-permute-done.1 = bf16[256,13056]{1,0:T(8,128)(2,1)} collective-permute-done((bf16[256,13056]{1,0:T(8,128)(2,1)}, bf16[256,13056]{1,0:T(8,128)(2,1)}, u32[]{:S(2)}, u32[]{:S(2)}) %collective-permute-start.1) | collective-permute-done | bytes 6684704 | tf_op jit(solution)/shard_map/ppermute | solution.py:19
  200.8 6.3 %collective-permute-done = bf16[256,13056]{1,0:T(8,128)(2,1)} collective-permute-done((bf16[256,13056]{1,0:T(8,128)(2,1)}, bf16[256,13056]{1,0:T(8,128)(2,1)}, u32[]{:S(2)}, u32[]{:S(2)}) %collective-permute-start) | collective-permute-done | bytes 6684704 | tf_op jit(solution)/shard_map/ppermute | solution.py:16
  207.1 14.6 %pad_maximum_fusion = bf16[768,13056]{1,0:T(8,128)(2,1)} fusion(bf16[256,13056]{1,0:T(8,128)(2,1)} %collective-permute-done.1, bf16[256,768]{1,0:T(8,128)(2,1)S(1)} %copy.13, bf16[256,12288]{1,0:T(8,128)(2,1)} %copy.12, bf16[256,13056]{1,0:T(8,128)(2,1)} %collective-permute-done), kind=kLoop, calls=%fused_computation | loop fusion | flops 80216064 | bytes 40108032 | tf_op jit(solution)/shard_map/concatenate | solution.py:20
  221.7 13.9 %constant_dynamic-slice_fusion.2 = (bf16[256,12288]{1,0:T(8,128)(2,1)}, bf16[256,12288]{1,0:T(8,128)(2,1)}, bf16[256,12288]{1,0:T(8,128)(2,1)}) fusion(bf16[768,13056]{1,0:T(8,128)(2,1)} %pad_maximum_fusion, s32[]{:T(128)S(6)} %select_n.32, s32[]{:T(128)S(6)} %select_n.36, s32[]{:T(128)S(6)} %select_n.34), kind=kLoop, calls=%fused_computation.30 | loop fusion | bytes 37748748 | tf_op jit(solution)/shard_map/slice | solution.py:38
  235.6 8.6 %copy.14 = bf16[256,12288]{0,1:T(8,128)(2,1)} copy(bf16[256,12288]{1,0:T(8,128)(2,1)} %get-tuple-element.6) | data formatting | bytes 12582912 | tf_op jit(solution)/shard_map/slice | solution.py:38
  248.9 4.9 %fusion.3 = bf16[256,3,4096]{2,0,1:T(8,128)(2,1)} fusion(s32[]{:T(128)S(6)} %select_n.43, bf16[256,3,4096]{2,0,1:T(8,128)(2,1)S(1)} %convolution_convert_fusion.2), kind=kLoop, calls=%fused_computation.15 | loop fusion | flops 12582912 | bytes 12582916 | tf_op jit(solution)/shard_map/jit(_roll_dynamic)/concatenate | solution.py:43
  253.9 8.6 %copy.16 = bf16[256,3,4096]{0,2,1:T(8,128)(2,1)} copy(bf16[256,3,4096]{2,0,1:T(8,128)(2,1)} %fusion.3) | data formatting | bytes 12582912 | tf_op jit(solution)/shard_map/jit(_roll_dynamic)/dynamic_slice | solution.py:43
  262.5 8.6 %copy.23 = bf16[256,12288]{0,1:T(8,128)(2,1)} copy(bf16[256,12288]{1,0:T(8,128)(2,1)} %get-tuple-element.7) | data formatting | bytes 12582912 | tf_op jit(solution)/shard_map/slice | solution.py:38
  271.1 4.7 %convolution_convert_fusion = bf16[256,3,4096]{2,0,1:T(8,128)(2,1)S(1)} fusion(bf16[256,3,4096]{0,2,1:T(8,128)(2,1)} %bitcast.52, bf16[768,13056]{1,0:T(8,128)(2,1)} %pad_maximum_fusion, s32[]{:T(128)S(6)} %select_n.36, s32[]{:T(128)S(6)} %add.88), kind=kOutput, calls=%fused_computation.8 | convolution fusion | flops 1613758464 | bytes 12713992 | tf_op jit(solution)/shard_map/ij,jvn->ivn/dot_general | solution.py:40
  275.8 5.0 %fusion.1 = bf16[256,3,4096]{2,0,1:T(8,128)(2,1)} fusion(s32[]{:T(128)S(6)} %select_n.47, bf16[256,3,4096]{2,0,1:T(8,128)(2,1)S(1)} %convolution_convert_fusion), kind=kLoop, calls=%fused_computation.13 | loop fusion | flops 12582912 | bytes 12582916 | tf_op jit(solution)/shard_map/jit(_roll_dynamic)/concatenate | solution.py:43
  280.8 8.6 %copy.25 = bf16[256,3,4096]{0,2,1:T(8,128)(2,1)} copy(bf16[256,3,4096]{2,0,1:T(8,128)(2,1)} %fusion.1) | data formatting | bytes 12582912 | tf_op jit(solution)/shard_map/jit(_roll_dynamic)/dynamic_slice | solution.py:43
  289.4 8.6 %copy.19 = bf16[256,12288]{0,1:T(8,128)(2,1)} copy(bf16[256,12288]{1,0:T(8,128)(2,1)} %get-tuple-element.8) | data formatting | bytes 12582912 | tf_op jit(solution)/shard_map/slice | solution.py:38
  298.0 4.7 %convolution_convert_fusion.1 = bf16[256,3,4096]{2,0,1:T(8,128)(2,1)S(1)} fusion(bf16[256,3,4096]{0,2,1:T(8,128)(2,1)} %bitcast.50, bf16[768,13056]{1,0:T(8,128)(2,1)} %pad_maximum_fusion, s32[]{:T(128)S(6)} %select_n.34, s32[]{:T(128)S(6)} %add.87), kind=kOutput, calls=%fused_computation.9 | convolution fusion | flops 1613758464 | bytes 12713992 | tf_op jit(solution)/shard_map/ij,jvn->ivn/dot_general | solution.py:40
  302.7 5.1 %fusion.2 = bf16[256,3,4096]{2,0,1:T(8,128)(2,1)} fusion(s32[]{:T(128)S(6)} %select_n.45, bf16[256,3,4096]{2,0,1:T(8,128)(2,1)S(1)} %convolution_convert_fusion.1), kind=kLoop, calls=%fused_computation.14 | loop fusion | flops 12582912 | bytes 12582916 | tf_op jit(solution)/shard_map/jit(_roll_dynamic)/concatenate | solution.py:43
  307.8 8.7 %copy.21 = bf16[256,3,4096]{0,2,1:T(8,128)(2,1)} copy(bf16[256,3,4096]{2,0,1:T(8,128)(2,1)} %fusion.2) | data formatting | bytes 12582912 | tf_op jit(solution)/shard_map/jit(_roll_dynamic)/dynamic_slice | solution.py:43
  316.5 9.6 %fusion.4 = f32[32,256,3,128]{1,3,2,0:T(8,128)} fusion(bf16[256,3,32,128]{0,3,2,1:T(8,128)(2,1)} %bitcast.47, bf16[3,32,128,128]{2,3,1,0:T(8,128)(2,1)} %all-gather.2.cloned.1.call-done), kind=kOutput, calls=%fused_computation.16 | convolution fusion | flops 805306368 | bytes 19922944 | tf_op jit(solution)/shard_map/ivrk,rkm->ivrm/dot_general | solution.py:44
  326.1 7.7 %fusion.6 = f32[32,256,3,128]{1,3,2,0:T(8,128)} fusion(bf16[256,3,32,128]{0,3,2,1:T(8,128)(2,1)S(1)} %bitcast.49, bf16[3,32,128,128]{2,3,1,0:T(8,128)(2,1)} %all-gather.2.cloned.1.call-done), kind=kOutput, calls=%fused_computation.18 | convolution fusion | flops 805306368 | bytes 19922944 | tf_op jit(solution)/shard_map/ivrk,rkm->ivrm/dot_general | solution.py:44
  333.8 13.1 %fusion = bf16[256,3,32,128]{0,3,1,2:T(8,128)(2,1)} fusion(f32[32,256,3,128]{1,3,2,0:T(8,128)} %fusion.4, f32[32,256,3,128]{1,3,2,0:T(8,128)} %fusion.6, pred[32]{0:T(512)(128)(4,1)S(1)} %get-tuple-element.12, pred[32]{0:T(512)(128)(4,1)S(1)} %get-tuple-element.13, pred[32]{0:T(512)(128)(4,1)S(1)} %compare_and_fusion.2, ...), kind=kOutput, calls=%fused_computation.12 | convolution fusion | flops 824180736 | bytes 38797408 | tf_op jit(solution)/shard_map/ivrk,rkm->ivrm/dot_general | solution.py:44
  346.9 6.2 %copy.27 = bf16[256,3,32,128]{0,3,2,1:T(8,128)(2,1)} copy(bf16[256,3,32,128]{0,3,1,2:T(8,128)(2,1)} %fusion) | data formatting | bytes 12582912 | tf_op jit(solution)/shard_map/convert_element_type | solution.py:50
  353.1 42.3 %reduce-scatter.2.cloned.1.call-done = bf16[256,3,512]{0,2,1:T(8,128)(2,1)} async-done(((bf16[256,3,4096]{0,2,1:T(8,128)(2,1)}), bf16[256,3,512]{0,2,1:T(8,128)(2,1)}) %reduce-scatter.2.cloned.1.call-update) | async-done | bytes 786448 | tf_op jit(solution)/shard_map/reduce_scatter | solution.py:51
  (25 shorter events, 13.5 us)
Async XLA Ops:
  6.5 310.0 %all-gather.2.cloned.1.call-start = ((), (), s32[]{:S(2)}) async-start(), calls=%async_computation.1 | async-start | bytes 3244032 | tf_op jit(solution)/shard_map/all_gather | solution.py:32
  25.2 15.7 %copy-start.1 = (bf16[3,1,128,128]{3,2,1,0:T(8,128)(2,1)S(1)}, bf16[3,1,128,128]{3,2,1,0:T(8,128)(2,1)}, u32[]{:S(2)}) copy-start(bf16[3,1,128,128]{3,2,1,0:T(8,128)(2,1)} %param.8) | copy-start | bytes 294916
  25.2 16.5 %copy-start.2 = (s32[3]{0:T(128)S(1)}, s32[3]{0:T(128)}, u32[]{:S(2)}) copy-start(s32[3]{0:T(128)} %param.9) | copy-start | bytes 40
  31.3 169.6 %collective-permute-start.1 = (bf16[256,13056]{1,0:T(8,128)(2,1)}, bf16[256,13056]{1,0:T(8,128)(2,1)}, u32[]{:S(2)}, u32[]{:S(2)}) collective-permute-start(bf16[256,13056]{1,0:T(8,128)(2,1)} %pad_maximum_fusion.1), channel_id=1, source_target_pairs={{1,0},{2,1},{3,2},{4,3},{5,4},{6,5},{7,6},{8,7},{9,8},{10,9},{11,1... | collective-permute-start | bytes 20054024 | tf_op jit(solution)/shard_map/ppermute | solution.py:19
  38.9 168.2 %collective-permute-start = (bf16[256,13056]{1,0:T(8,128)(2,1)}, bf16[256,13056]{1,0:T(8,128)(2,1)}, u32[]{:S(2)}, u32[]{:S(2)}) collective-permute-start(bf16[256,13056]{1,0:T(8,128)(2,1)} %pad_maximum_fusion.1), channel_id=1, source_target_pairs={{0,1},{1,2},{2,3},{3,4},{4,5},{5,6},{6,7},{7,8},{8,9},{9,10},{10,1... | collective-permute-start | bytes 20054024 | tf_op jit(solution)/shard_map/ppermute | solution.py:16
  41.6 353.8 %reduce-scatter.2.cloned.1.call-start = ((), (), s32[]{:S(2)}) async-start(), calls=%async_computation.2 | async-start | bytes 7077888 | tf_op jit(solution)/shard_map/reduce_scatter | solution.py:51
  316.5 9.6 %copy-start = (bf16[256,3,4096]{0,2,1:T(8,128)(2,1)S(1)}, bf16[256,3,4096]{0,2,1:T(8,128)(2,1)}, u32[]{:S(2)}) copy-start(bf16[256,3,4096]{0,2,1:T(8,128)(2,1)} %copy.21) | copy-start | bytes 18874372
  316.5 17.3 %slice-start = ((s8[6291456]{0:T(1024)(128)(4,1)}), s8[4194304]{0:T(1024)(128)(4,1)S(1)}, s32[]{:S(2)}) async-start(s8[6291456]{0:T(1024)(128)(4,1)} %bitcast.44), calls=%async_computation.3 | async-start | bytes 8388608
  326.1 7.7 %slice-start.1 = ((s8[6291456]{0:T(1024)(128)(4,1)}), s8[2097152]{0:T(1024)(128)(4,1)S(1)}, s32[]{:S(2)}) async-start(s8[6291456]{0:T(1024)(128)(4,1)} %bitcast.44), calls=%async_computation.4 | async-start | bytes 4194304
Sparse Core Ops, SparseCore 0:
  41.8 124.1 all-gather.1
  353.3 42.1 reduce-scatter.1
where the time goes:
time: 407 us; the launch traced here: 405 us
  waiting for transfers between devices  202 us (50%)
  local copies, waits for them, and re-layouts  94.2 us (23%)
  matrix products  44.4 us (11%)
  other arithmetic  37.5 us (9%)
  between operations  17.2 us (4%)
  starting transfers between devices  9.61 us (2%)
    ppermute x1, waiting for transfers between devices, extended(): lax.ppermute(lax.slice_in_dim(block, 0, width, axis=dim), axis, backward)  153 us
    reduce_scatter x1, waiting for transfers between devices, on_device(): lax.psum_scatter(row_layout.astype(jnp.float32).astype(jnp.bfloat16), 'op...  42.3 us
    slice x4, local copies, waits for them, and re-layouts, on_device(): source = rows_block[:, :VECS * columns].reshape(ML, VECS, columns)  39.7 us
    dot_general x3, matrix products, on_device(): jnp.einsum('ivrk,rkm->ivrm', rolled, right_all[inner], preferred_element_...  30.3 us
    dynamic_slice x3, local copies, waits for them, and re-layouts, on_device(): jnp.roll(product, -offset * MR, axis=2).reshape(ML, VECS, right_count, MR)  26 us
    concatenate x3, other arithmetic, on_device(): jnp.roll(product, -offset * MR, axis=2).reshape(ML, VECS, right_count, MR)  15 us
    concatenate x1, other arithmetic, extended(): block = jnp.concatenate([low, block, high], axis=dim)  14.6 us
    dot_general x3, matrix products, on_device(): jnp.einsum('ij,jvn->ivn', left_block, source, preferred_element_type=jnp....  14.1 us
  transfers between devices with their start and end apart: 4, of which 3 were waited for; matrix products, arithmetic and copies ran while one was open for 28% of the time, Pallas kernels for 0%

commit v1 on v0

v1 whole, which is shorter than its diff:
```python
import functools

import jax
import jax.numpy as jnp
from jax import lax
from jax.experimental import pallas as pl
from jax.experimental.pallas import tpu as pltpu
from jax.sharding import PartitionSpec as P

X, CORES, Y, Z = 4, 2, 4, 8
GROUPS = X * CORES
SECTORS = Y * Z
OWN = SECTORS // GROUPS
MESH = pl.DeviceIdType.MESH


def kernel(
    w_hbm, l_hbm, r_hbm, sh_in, out,
    w, l, r, z, rm, acc, sbuf, rbuf, shv, shs,
    loc, ps, pr, zs, zr, ys, yr, ls, lr, ss, sr, os_, or_,
):
    op, sec = lax.axis_index("op"), lax.axis_index("sec")
    xx, core = lax.div(op, CORES), lax.rem(op, CORES)
    yy, zz = lax.div(sec, Z), lax.rem(sec, Z)
    vecs, ml, mr = w.shape[1], w.shape[2], w.shape[3]
    terms = l.shape[1]
    half = ml // 2

    def group(dx, other=0):
        return lax.rem(xx + dx + X, X) * CORES + (lax.rem(core + other, CORES))

    def z_of(d):
        return lax.rem(zz + d + Z, Z)

    def y_of(d):
        return lax.rem(yy + d + Y, Y)

    x_up, x_dn, sib = (group(1), sec), (group(-1), sec), (group(0, 1), sec)
    z_up, z_dn = (op, yy * Z + z_of(1)), (op, yy * Z + z_of(-1))
    y_up, y_dn = (op, y_of(1) * Z + zz), (op, y_of(-1) * Z + zz)
    s_up = (op, lax.rem(sec + 1, SECTORS))
    s_dn = (op, lax.rem(sec + SECTORS - 1, SECTORS))
    to_op, to_sec = lax.div(sec, OWN), xx * Z + lax.rem(sec, OWN) * CORES + core
    from_op = yy * CORES + lax.rem(zz, CORES)
    from_sec = op * OWN + lax.div(zz, CORES)
    stays = (to_op == op) & (to_sec == sec)
    moves = jnp.logical_not(stays)

    first = op * OWN - 1
    for k in range(OWN + 2):
        def load(k=k):
            at = pl.multiple_of((first + k) * mr, mr)
            pltpu.make_async_copy(w_hbm.at[:, :, pl.ds(at, mr)], w.at[k], loc.at[k]).start()

        def blank(k=k):
            w[k] = jnp.zeros(w.shape[1:], w.dtype)

        if k == 0:
            pl.when(op > 0)(load)
            pl.when(op == 0)(blank)
        elif k == OWN + 1:
            pl.when(op < GROUPS - 1)(load)
            pl.when(op == GROUPS - 1)(blank)
        else:
            load()
    own_l = pltpu.make_async_copy(l_hbm, l.at[op], loc.at[OWN + 2])
    own_l.start()
    own_sh = pltpu.make_async_copy(sh_in, shv.at[op], loc.at[OWN + 3])
    own_sh.start()

    barrier = pltpu.get_barrier_semaphore()
    greet = [z_up, z_dn, y_up, y_dn, s_up, s_dn]
    greet += [(lax.rem(op + d, GROUPS), sec) for d in range(1, GROUPS)]
    for who in greet:
        pl.semaphore_signal(barrier, inc=1, device_id=who, device_id_type=MESH)

    @pl.when(moves)
    def _():
        for who in ((to_op, to_sec), (from_op, from_sec)):
            pl.semaphore_signal(barrier, inc=1, device_id=who, device_id_type=MESH)
        pl.semaphore_wait(barrier, len(greet) + 2)

    @pl.when(stays)
    def _():
        pl.semaphore_wait(barrier, len(greet))

    sent = []

    def copy(src, dst, send, recv, who):
        return pltpu.make_async_remote_copy(
            src_ref=src, dst_ref=dst, send_sem=send, recv_sem=recv, device_id=who, device_id_type=MESH
        )

    def push(src, dst, send, recv, who):
        c = copy(src, dst, send, recv, who)
        c.start()
        sent.append(c)

    def got(dst, send, recv, who):
        copy(dst, dst, send, recv, who).wait_recv()

    @pl.when(moves)
    def _():
        copy(r_hbm, r.at[xx, lax.rem(sec, OWN) * CORES + core], ps.at[0], pr.at[0], (to_op, to_sec)).start()

    @pl.when(stays)
    def _():
        pltpu.make_async_copy(r_hbm, r.at[yy, zz], loc.at[OWN + 4]).start()

    for d in range(1, GROUPS):
        push(sh_in, shv.at[op], ss.at[d], sr.at[op], (lax.rem(op + d, GROUPS), sec))
    push(l_hbm, l.at[op], ls.at[2], lr.at[2], sib)
    push(l_hbm, l.at[op], ls.at[0], lr.at[0], x_up)
    push(l_hbm, l.at[op], ls.at[1], lr.at[1], x_dn)

    def row_send(c):
        blk = r.at[yy, c]
        push(blk, blk, ys.at[0, c], yr.at[0, c], y_up)
        push(blk, blk, ys.at[1, c], yr.at[1, c], y_dn)

    def row_forward(sigma):
        a, b = sigma * CORES, sigma * CORES + 1
        low, high = r.at[y_of(-1), a], r.at[y_of(1), b]
        got(low, ys.at[0, a], yr.at[0, a], y_dn)
        push(low, low, ys.at[2, a], yr.at[2, a], y_up)
        got(high, ys.at[1, b], yr.at[1, b], y_up)
        push(high, high, ys.at[2, b], yr.at[2, b], y_dn)

    def row_finish(sigma):
        a, b = sigma * CORES, sigma * CORES + 1
        got(r.at[y_of(1), a], ys.at[1, a], yr.at[1, a], y_up)
        got(r.at[y_of(-1), b], ys.at[0, b], yr.at[0, b], y_dn)
        got(r.at[y_of(2), a], ys.at[2, a], yr.at[2, a], y_dn)
        got(r.at[y_of(2), b], ys.at[2, b], yr.at[2, b], y_up)

    def hop_up(k):
        blk = r.at[yy, z_of(-k)]
        push(blk, blk, zs.at[k], zr.at[k], z_up)

    def hop_dn(k):
        blk = r.at[yy, z_of(k)]
        push(blk, blk, zs.at[4 + k], zr.at[4 + k], z_dn)

    def hop_got(k):
        got(r.at[yy, z_of(-k)], zs.at[k - 1], zr.at[k - 1], z_dn)
        if k < 4:
            got(r.at[yy, z_of(k)], zs.at[3 + k], zr.at[3 + k], z_up)

    def left_products(g):
        def one(i, carry):
            s = shs[g, 0, i]
            cols = jnp.concatenate(
                [w[s + 1 + b, v] for b in range(OWN) for v in range(vecs)], axis=1
            )
            prod = jnp.dot(l[g, i], cols, preferred_element_type=jnp.float32).astype(z.dtype)
            for b in range(OWN):
                for v in range(vecs):
                    n = b * vecs + v
                    z[b, v, g * terms + i] = prod[:, n * mr : (n + 1) * mr]
            return carry

        lax.fori_loop(0, terms, one, 0)

    def right_products(sigma):
        for g in range(GROUPS):
            for i in range(terms):
                s = shs[g, 0, i]
                blk = r[g // CORES, sigma * CORES + g % CORES, i]
                for q in range(3):
                    kept = jnp.where(jnp.full(blk.shape, s, jnp.int32) == q - 1, blk, jnp.zeros_like(blk))
                    rm[g * terms + i, :, q * mr : (q + 1) * mr] = kept

        def one(v, carry):
            lhs = jnp.concatenate([z[sigma, v, t] for t in range(GROUPS * terms)], axis=1)
            rhs = rm[...].reshape(GROUPS * terms * mr, 3 * mr)
            sums = jnp.dot(lhs, rhs, preferred_element_type=jnp.float32)
            sbuf[0, sigma, v] = sums[:, :mr].astype(sbuf.dtype)
            acc[sigma, v] = sums[:, mr : 2 * mr]
            sbuf[1, sigma, v] = sums[:, 2 * mr :].astype(sbuf.dtype)
            for q, who in ((0, s_dn), (1, s_up)):
                copy(sbuf.at[q, sigma, v], rbuf.at[q, sigma, v], os_.at[q, sigma, v], or_.at[q, sigma, v], who).start()
            return carry

        lax.fori_loop(0, vecs, one, 0)

    @pl.when(moves)
    def _():
        got(r.at[yy, zz], ps.at[0], pr.at[0], (from_op, from_sec))

    @pl.when(stays)
    def _():
        pltpu.make_async_copy(r_hbm, r.at[yy, zz], loc.at[OWN + 4]).wait()

    hop_up(0)
    hop_dn(0)
    row_send(zz)

    turn = 1 - 2 * lax.rem(zz, 2)
    s0 = lax.div(zz, CORES)
    order = [s0, lax.rem(s0 - turn + OWN, OWN), lax.rem(s0 + turn + OWN, OWN), lax.rem(s0 + 2, OWN)]

    own_sh.wait()
    for d in range(1, GROUPS):
        g = lax.rem(op + d, GROUPS)
        got(shv.at[g], ss.at[GROUPS - d], sr.at[g], (g, sec))
    shift_in = pltpu.make_async_copy(shv, shs, loc.at[OWN + 5])
    shift_in.start()
    shift_in.wait()
    own_l.wait()
    for k in range(OWN + 2):
        def arrived(k=k):
            pltpu.make_async_copy(w_hbm.at[:, :, pl.ds(0, mr)], w.at[k], loc.at[k]).wait()

        if k == 0:
            pl.when(op > 0)(arrived)
        elif k == OWN + 1:
            pl.when(op < GROUPS - 1)(arrived)
        else:
            arrived()
    left_products(op)

    hop_got(1)
    hop_up(1)
    hop_dn(1)
    row_send(z_of(turn))

    got(l.at[group(0, 1)], ls.at[2], lr.at[2], sib)
    left_products(group(0, 1))

    g_dn, g_up, g_far = group(-1), group(1), group(2)
    got(l.at[g_dn], ls.at[0], lr.at[0], x_dn)
    push(l.at[g_dn, :, :half], l.at[g_dn, :, :half], ls.at[5], lr.at[5], x_up)
    push(l.at[g_dn], l.at[g_dn], ls.at[3], lr.at[3], sib)
    got(l.at[g_up], ls.at[1], lr.at[1], x_up)
    push(l.at[g_up, :, half:], l.at[g_up, :, half:], ls.at[6], lr.at[6], x_dn)
    push(l.at[g_up], l.at[g_up], ls.at[4], lr.at[4], sib)

    hop_got(2)
    hop_up(2)
    hop_dn(2)
    row_send(order[1] * CORES)
    row_send(order[1] * CORES + 1)
    row_forward(order[0])

    left_products(g_dn)
    left_products(g_up)

    hop_got(3)
    hop_up(3)
    row_send(order[2] * CORES)
    row_send(order[2] * CORES + 1)
    row_forward(order[1])

    got(l.at[g_far, :, :half], ls.at[5], lr.at[5], x_dn)
    push(l.at[g_far, :, :half], l.at[g_far, :, :half], ls.at[7], lr.at[7], sib)
    got(l.at[g_far, :, half:], ls.at[6], lr.at[6], x_up)
    push(l.at[g_far, :, half:], l.at[g_far, :, half:], ls.at[8], lr.at[8], sib)
    got(l.at[group(-1, 1)], ls.at[3], lr.at[3], sib)
    left_products(group(-1, 1))
    got(l.at[group(1, 1)], ls.at[4], lr.at[4], sib)
    left_products(group(1, 1))

    hop_got(4)
    row_send(order[3] * CORES)
    row_send(order[3] * CORES + 1)
    row_forward(order[2])

    left_products(g_far)
    got(l.at[group(2, 1), :, :half], ls.at[7], lr.at[7], sib)
    got(l.at[group(2, 1), :, half:], ls.at[8], lr.at[8], sib)
    left_products(group(2, 1))

    row_finish(order[0])
    right_products(order[0])
    row_forward(order[3])
    for sigma in order[1:]:
        row_finish(sigma)
        right_products(sigma)

    def total(sigma, carry):
        for v in range(vecs):
            got(rbuf.at[0, sigma, v], os_.at[0, sigma, v], or_.at[0, sigma, v], s_up)
            got(rbuf.at[1, sigma, v], os_.at[1, sigma, v], or_.at[1, sigma, v], s_dn)
        for v in range(vecs):
            above = rbuf[0, sigma, v].astype(jnp.float32)
            below = rbuf[1, sigma, v].astype(jnp.float32)
            whole = acc[sigma, v]
            whole = whole + jnp.where(jnp.full(above.shape, sec, jnp.int32) < SECTORS - 1, above, 0.0)
            whole = whole + jnp.where(jnp.full(below.shape, sec, jnp.int32) > 0, below, 0.0)
            at = pl.multiple_of(sigma * mr, mr)
            out[v, :, pl.ds(at, mr)] = whole.astype(out.dtype)
        return carry

    lax.fori_loop(0, OWN, total, 0)

    for c in sent:
        c.wait_send()

    @pl.when(moves)
    def _():
        copy(r_hbm, r.at[xx, lax.rem(sec, OWN) * CORES + core], ps.at[0], pr.at[0], (to_op, to_sec)).wait_send()

    def drain(sigma, carry):
        for v in range(vecs):
            for q, who in ((0, s_dn), (1, s_up)):
                copy(
                    sbuf.at[q, sigma, v], rbuf.at[q, sigma, v], os_.at[q, sigma, v], or_.at[q, sigma, v], who
                ).wait_send()
        return carry

    lax.fori_loop(0, OWN, drain, 0)


def on_device(wavefunction, left_ops, right_ops, term_shift):
    ml, vecs, _ = wavefunction.shape
    terms, mr = left_ops.shape[1], right_ops.shape[2]
    shifts = jnp.pad(term_shift.reshape(1, terms), ((0, 7), (0, 128 - terms)))
    every = GROUPS * terms
    flops = 2 * every * ml * ml * vecs * OWN * mr + 2 * every * vecs * ml * mr * OWN * mr
    anywhere = pl.BlockSpec(memory_space=pl.ANY)
    dma = pltpu.SemaphoreType.DMA
    bf16 = wavefunction.dtype
    result = pl.pallas_call(
        kernel,
        out_shape=jax.ShapeDtypeStruct((vecs, ml, OWN * mr), bf16),
        in_specs=[anywhere, anywhere, anywhere, anywhere],
        out_specs=pl.BlockSpec(memory_space=pltpu.VMEM),
        scratch_shapes=[
            pltpu.VMEM((OWN + 2, vecs, ml, mr), bf16),
            pltpu.VMEM((GROUPS, terms, ml, ml), bf16),
            pltpu.VMEM((Y, Z, terms, mr, mr), bf16),
            pltpu.VMEM((OWN, vecs, every, ml, mr), bf16),
            pltpu.VMEM((every, mr, 3 * mr), bf16),
            pltpu.VMEM((OWN, vecs, ml, mr), jnp.float32),
            pltpu.VMEM((2, OWN, vecs, ml, mr), bf16),
            pltpu.VMEM((2, OWN, vecs, ml, mr), bf16),
            pltpu.VMEM((GROUPS, 8, 128), jnp.int32),
            pltpu.SMEM((GROUPS, 8, 128), jnp.int32),
            dma((OWN + 6,)),
            dma((1,)), dma((1,)),
            dma((7,)), dma((7,)),
            dma((3, Z)), dma((3, Z)),
            dma((9,)), dma((9,)),
            dma((GROUPS,)), dma((GROUPS,)),
            dma((2, OWN, vecs)), dma((2, OWN, vecs)),
        ],
        compiler_params=pltpu.CompilerParams(
            collective_id=0, has_side_effects=True, vmem_limit_bytes=56 * 2**20
        ),
        cost_estimate=pl.CostEstimate(flops=flops, bytes_accessed=4 * 2**20, transcendentals=0),
    )(
        jnp.transpose(wavefunction, (1, 0, 2)),
        jnp.transpose(left_ops, (1, 0, 2)),
        right_ops.reshape(terms, mr, mr),
        shifts,
    )
    return jnp.transpose(result, (1, 0, 2))


def solution(mesh):
    in_specs = (P("sec", None, None), P("sec", "op", None), P("op", "sec", None, None), P("op"))
    out_specs = P("sec", None, "op")
    return jax.shard_map(
        on_device, mesh=mesh, in_specs=in_specs, out_specs=out_specs, check_vma=False
    )
```

time: 407 us -> 82.7 us (0.20)
  waiting for transfers between devices: 202 us -> 0 us
  local copies, waits for them, and re-layouts: 94.2 us -> 3.31 us
  Pallas kernels: 0 us -> 77.8 us
  matrix products: 44.4 us -> 0 us
  other arithmetic: 37.5 us -> 0 us
  between operations: 17.2 us -> 0.01 us
  starting transfers between devices: 9.61 us -> 0 us
    ppermute x2 -> x0, waiting for transfers between devices: 159 us -> none  [the longest x1 153 us: extended(): lax.ppermute(lax.slice_in_dim(block, 0, width, axis=dim), axis, backward)]
    pallas_call x0 -> x1, Pallas kernels: none -> 77.8 us  [on_device(): pl.pallas_call(kernel, out_shape=jax.ShapeDtypeStruct((vecs, ml, OWN * mr...]
    dot_general x6 -> x0, matrix products: 44.4 us -> none  [the longest x3 30.3 us: on_device(): jnp.einsum('ivrk,rkm->ivrm', rolled, right_all[inner], preferred_element_...]
    reduce_scatter x1 -> x0, waiting for transfers between devices: 42.3 us -> none  [on_device(): lax.psum_scatter(row_layout.astype(jnp.float32).astype(jnp.bfloat16), 'op...]
    slice x5 -> x0, local copies, waits for them, and re-layouts: 40.3 us -> none  [the longest x4 39.7 us: on_device(): source = rows_block[:, :VECS * columns].reshape(ML, VECS, columns)]
    concatenate x5 -> x0, other arithmetic: 35.7 us -> none  [the longest x3 15 us: on_device(): jnp.roll(product, -offset * MR, axis=2).reshape(ML, VECS, right_count, MR)]
    dynamic_slice x3 -> x0, local copies, waits for them, and re-layouts: 26 us -> none  [on_device(): jnp.roll(product, -offset * MR, axis=2).reshape(ML, VECS, right_count, MR)]
    ppermute x2 -> x0, starting transfers between devices: 9.56 us -> none  [the longest x1 7.64 us: extended(): lax.ppermute(lax.slice_in_dim(block, 0, width, axis=dim), axis, backward)]
  transfers between devices with their start and end apart: 4 -> 0, of which waited for: 3 -> 0; matrix products, arithmetic and copies ran while one was open for 28% -> 0% of each run, Pallas kernels for 0% -> 0%
where the time goes in v1:
time: 82.7 us; the launch traced here: 81.1 us
  Pallas kernels  77.8 us (94%)
  local copies, waits for them, and re-layouts  3.31 us (4%)
    pallas_call x1, Pallas kernels, on_device(): pl.pallas_call(kernel, out_shape=jax.ShapeDtypeStruct((vecs, ml, OWN * mr...  77.8 us
    unnamed x1, local copies, waits for them, and re-layouts  2.06 us

profile of v1, /device:TPU:16, one launch (start us, length us, event | category | flops | bytes accessed | tf_op | source)
XLA Modules:
  0.0 81.1 jit_solution(7981331383133249800)
XLA Ops:
  0.0 1.3 %pad.4.sh_in = s32[8,128]{1,0:T(8,128)} pad(s32[1,3]{1,0:T(1,128)} %bitcast.6, s32[]{:T(128)} %constant.0.clone.1), padding=0_7x0_125 | pad | bytes 4112 | tf_op jit(solution)/shard_map/jit(_pad)/pad | solution.py:317
  1.3 77.8 %shard_map.46 = bf16[3,256,512]{2,1,0:T(8,128)(2,1)} custom-call(bf16[3,256,4096]{2,1,0:T(8,128)(2,1)} %bitcast.7, bf16[3,256,256]{2,1,0:T(8,128)(2,1)} %bitcast.8, bf16[3,128,128]{2,1,0:T(8,128)(2,1)} %bitcast.9, s32[8,128]{1,0:T(8,128)} %pad.4.sh_in), custom_call_target="tpu_custom_call" | custom-call | flops 7247757312 | bytes 4194304 | tf_op jit(solution)/shard_map/pallas_call | solution.py:323
  79.0 2.1 %copy.6 = bf16[256,3,512]{2,0,1:T(8,128)(2,1)} copy(bf16[256,3,512]{2,0,1:T(8,128)(2,1)} %bitcast.5) | data formatting | bytes 1572864

commit v2 on v1

--- a/solution.py
+++ b/solution.py
@@ -40,9 +40,20 @@
     y_up, y_dn = (op, y_of(1) * Z + zz), (op, y_of(-1) * Z + zz)
     s_up = (op, lax.rem(sec + 1, SECTORS))
     s_dn = (op, lax.rem(sec + SECTORS - 1, SECTORS))
-    to_op, to_sec = lax.div(sec, OWN), xx * Z + lax.rem(sec, OWN) * CORES + core
-    from_op = yy * CORES + lax.rem(zz, CORES)
-    from_sec = op * OWN + lax.div(zz, CORES)
+    def pair_of(n, c):
+        return lax.rem(n + OWN - 1 + 2 * c, OWN)
+
+    def sector_of(p):
+        return lax.rem(p + 1 + 2 * core, OWN)
+
+    def far_y(d):
+        return lax.rem(d + 2, Y)
+
+    to_op = lax.div(sec, OWN)
+    to_y, to_z = far_y(xx), pair_of(lax.rem(sec, OWN), lax.rem(to_op, CORES)) * CORES + core
+    to_sec = to_y * Z + to_z
+    from_op = far_y(yy) * CORES + lax.rem(zz, CORES)
+    from_sec = op * OWN + sector_of(lax.div(zz, CORES))
     stays = (to_op == op) & (to_sec == sec)
     moves = jnp.logical_not(stays)
 
@@ -65,8 +76,11 @@
             load()
     own_l = pltpu.make_async_copy(l_hbm, l.at[op], loc.at[OWN + 2])
     own_l.start()
-    own_sh = pltpu.make_async_copy(sh_in, shv.at[op], loc.at[OWN + 3])
-    own_sh.start()
+    lane = lax.broadcasted_iota(jnp.int32, shv.shape[1:], 1)
+    own_shifts = jnp.zeros(shv.shape[1:], jnp.int32)
+    for i in range(terms):
+        own_shifts = jnp.where(lane == i, jnp.full(lane.shape, sh_in[i], jnp.int32), own_shifts)
+    shv[op] = own_shifts
 
     barrier = pltpu.get_barrier_semaphore()
     greet = [z_up, z_dn, y_up, y_dn, s_up, s_dn]
@@ -101,14 +115,15 @@
 
     @pl.when(moves)
     def _():
-        copy(r_hbm, r.at[xx, lax.rem(sec, OWN) * CORES + core], ps.at[0], pr.at[0], (to_op, to_sec)).start()
+        for i in range(terms):
+            copy(r_hbm.at[i], r.at[to_y, to_z, i], ps.at[i], pr.at[i], (to_op, to_sec)).start()
 
     @pl.when(stays)
     def _():
         pltpu.make_async_copy(r_hbm, r.at[yy, zz], loc.at[OWN + 4]).start()
 
     for d in range(1, GROUPS):
-        push(sh_in, shv.at[op], ss.at[d], sr.at[op], (lax.rem(op + d, GROUPS), sec))
+        push(shv.at[op], shv.at[op], ss.at[d], sr.at[op], (lax.rem(op + d, GROUPS), sec))
     push(l_hbm, l.at[op], ls.at[2], lr.at[2], sib)
     push(l_hbm, l.at[op], ls.at[0], lr.at[0], x_up)
     push(l_hbm, l.at[op], ls.at[1], lr.at[1], x_dn)
@@ -118,33 +133,46 @@
         push(blk, blk, ys.at[0, c], yr.at[0, c], y_up)
         push(blk, blk, ys.at[1, c], yr.at[1, c], y_dn)
 
-    def row_forward(sigma):
-        a, b = sigma * CORES, sigma * CORES + 1
-        low, high = r.at[y_of(-1), a], r.at[y_of(1), b]
-        got(low, ys.at[0, a], yr.at[0, a], y_dn)
-        push(low, low, ys.at[2, a], yr.at[2, a], y_up)
-        got(high, ys.at[1, b], yr.at[1, b], y_up)
-        push(high, high, ys.at[2, b], yr.at[2, b], y_dn)
-
-    def row_finish(sigma):
-        a, b = sigma * CORES, sigma * CORES + 1
-        got(r.at[y_of(1), a], ys.at[1, a], yr.at[1, a], y_up)
-        got(r.at[y_of(-1), b], ys.at[0, b], yr.at[0, b], y_dn)
-        got(r.at[y_of(2), a], ys.at[2, a], yr.at[2, a], y_dn)
-        got(r.at[y_of(2), b], ys.at[2, b], yr.at[2, b], y_up)
-
-    def hop_up(k):
-        blk = r.at[yy, z_of(-k)]
-        push(blk, blk, zs.at[k], zr.at[k], z_up)
-
-    def hop_dn(k):
-        blk = r.at[yy, z_of(k)]
-        push(blk, blk, zs.at[4 + k], zr.at[4 + k], z_dn)
-
-    def hop_got(k):
-        got(r.at[yy, z_of(-k)], zs.at[k - 1], zr.at[k - 1], z_dn)
-        if k < 4:
-            got(r.at[yy, z_of(k)], zs.at[3 + k], zr.at[3 + k], z_up)
+    def passage(c):
+        if c:
+            upward = jnp.where(zz == Z - 1, 1, 0)
+        else:
+            upward = jnp.where(zz == 0, 0, 1)
+        to = (op, y_of(2 * upward - 1) * Z + zz)
+        source = (op, y_of(1 - 2 * upward) * Z + zz)
+        return 1 - upward, to, source
+
+    def row_forward(p):
+        for c in range(CORES):
+            at = p * CORES + c
+            way, to, source = passage(c)
+            blk = r.at[y_of(2 * way - 1), at]
+            got(blk, ys.at[way, at], yr.at[way, at], source)
+            push(blk, blk, ys.at[2, at], yr.at[2, at], to)
+
+    def row_finish(p):
+        for c in range(CORES):
+            at = p * CORES + c
+            way, to, source = passage(c)
+            got(r.at[y_of(1 - 2 * way), at], ys.at[1 - way, at], yr.at[1 - way, at], to)
+            got(r.at[y_of(2), at], ys.at[2, at], yr.at[2, at], source)
+
+    def hop_up(k, i):
+        blk = r.at[yy, z_of(-k), i]
+        push(blk, blk, zs.at[k, i], zr.at[k, i], z_up)
+
+    def hop_dn(k, i):
+        blk = r.at[yy, z_of(k), i]
+        push(blk, blk, zs.at[4 + k, i], zr.at[4 + k, i], z_dn)
+
+    def hop(k):
+        for i in range(terms):
+            got(r.at[yy, z_of(-k), i], zs.at[k - 1, i], zr.at[k - 1, i], z_dn)
+            if k < 4:
+                hop_up(k, i)
+                got(r.at[yy, z_of(k), i], zs.at[3 + k, i], zr.at[3 + k, i], z_up)
+            if k < 3:
+                hop_dn(k, i)
 
     def left_products(g):
         def one(i, carry):
@@ -161,11 +189,12 @@
 
         lax.fori_loop(0, terms, one, 0)
 
-    def right_products(sigma):
+    def right_products(p):
+        sigma = sector_of(p)
         for g in range(GROUPS):
             for i in range(terms):
                 s = shs[g, 0, i]
-                blk = r[g // CORES, sigma * CORES + g % CORES, i]
+                blk = r[(g // CORES + 2) % Y, p * CORES + g % CORES, i]
                 for q in range(3):
                     kept = jnp.where(jnp.full(blk.shape, s, jnp.int32) == q - 1, blk, jnp.zeros_like(blk))
                     rm[g * terms + i, :, q * mr : (q + 1) * mr] = kept
@@ -183,23 +212,23 @@
 
         lax.fori_loop(0, vecs, one, 0)
 
-    @pl.when(moves)
-    def _():
-        got(r.at[yy, zz], ps.at[0], pr.at[0], (from_op, from_sec))
-
     @pl.when(stays)
     def _():
         pltpu.make_async_copy(r_hbm, r.at[yy, zz], loc.at[OWN + 4]).wait()
 
-    hop_up(0)
-    hop_dn(0)
+    for i in range(terms):
+        @pl.when(moves)
+        def _(i=i):
+            got(r.at[yy, zz, i], ps.at[i], pr.at[i], (from_op, from_sec))
+
+        hop_up(0, i)
+        hop_dn(0, i)
     row_send(zz)
 
     turn = 1 - 2 * lax.rem(zz, 2)
     s0 = lax.div(zz, CORES)
     order = [s0, lax.rem(s0 - turn + OWN, OWN), lax.rem(s0 + turn + OWN, OWN), lax.rem(s0 + 2, OWN)]
 
-    own_sh.wait()
     for d in range(1, GROUPS):
         g = lax.rem(op + d, GROUPS)
         got(shv.at[g], ss.at[GROUPS - d], sr.at[g], (g, sec))
@@ -219,9 +248,7 @@
             arrived()
     left_products(op)
 
-    hop_got(1)
-    hop_up(1)
-    hop_dn(1)
+    hop(1)
     row_send(z_of(turn))
 
     got(l.at[group(0, 1)], ls.at[2], lr.at[2], sib)
@@ -235,9 +262,7 @@
     push(l.at[g_up, :, half:], l.at[g_up, :, half:], ls.at[6], lr.at[6], x_dn)
     push(l.at[g_up], l.at[g_up], ls.at[4], lr.at[4], sib)
 
-    hop_got(2)
-    hop_up(2)
-    hop_dn(2)
+    hop(2)
     row_send(order[1] * CORES)
     row_send(order[1] * CORES + 1)
     row_forward(order[0])
@@ -245,8 +270,7 @@
     left_products(g_dn)
     left_products(g_up)
 
-    hop_got(3)
-    hop_up(3)
+    hop(3)
     row_send(order[2] * CORES)
     row_send(order[2] * CORES + 1)
     row_forward(order[1])
@@ -260,7 +284,7 @@
     got(l.at[group(1, 1)], ls.at[4], lr.at[4], sib)
     left_products(group(1, 1))
 
-    hop_got(4)
+    hop(4)
     row_send(order[3] * CORES)
     row_send(order[3] * CORES + 1)
     row_forward(order[2])
@@ -273,9 +297,9 @@
     row_finish(order[0])
     right_products(order[0])
     row_forward(order[3])
-    for sigma in order[1:]:
-        row_finish(sigma)
-        right_products(sigma)
+    for p in order[1:]:
+        row_finish(p)
+        right_products(p)
 
     def total(sigma, carry):
         for v in range(vecs):
@@ -298,7 +322,8 @@
 
     @pl.when(moves)
     def _():
-        copy(r_hbm, r.at[xx, lax.rem(sec, OWN) * CORES + core], ps.at[0], pr.at[0], (to_op, to_sec)).wait_send()
+        for i in range(terms):
+            copy(r_hbm.at[i], r.at[to_y, to_z, i], ps.at[i], pr.at[i], (to_op, to_sec)).wait_send()
 
     def drain(sigma, carry):
         for v in range(vecs):
@@ -314,7 +339,6 @@
 def on_device(wavefunction, left_ops, right_ops, term_shift):
     ml, vecs, _ = wavefunction.shape
     terms, mr = left_ops.shape[1], right_ops.shape[2]
-    shifts = jnp.pad(term_shift.reshape(1, terms), ((0, 7), (0, 128 - terms)))
     every = GROUPS * terms
     flops = 2 * every * ml * ml * vecs * OWN * mr + 2 * every * vecs * ml * mr * OWN * mr
     anywhere = pl.BlockSpec(memory_space=pl.ANY)
@@ -323,7 +347,7 @@
     result = pl.pallas_call(
         kernel,
         out_shape=jax.ShapeDtypeStruct((vecs, ml, OWN * mr), bf16),
-        in_specs=[anywhere, anywhere, anywhere, anywhere],
+        in_specs=[anywhere, anywhere, anywhere, pl.BlockSpec(memory_space=pltpu.SMEM)],
         out_specs=pl.BlockSpec(memory_space=pltpu.VMEM),
         scratch_shapes=[
             pltpu.VMEM((OWN + 2, vecs, ml, mr), bf16),
@@ -337,8 +361,8 @@
             pltpu.VMEM((GROUPS, 8, 128), jnp.int32),
             pltpu.SMEM((GROUPS, 8, 128), jnp.int32),
             dma((OWN + 6,)),
-            dma((1,)), dma((1,)),
-            dma((7,)), dma((7,)),
+            dma((terms,)), dma((terms,)),
+            dma((7, terms)), dma((7, terms)),
             dma((3, Z)), dma((3, Z)),
             dma((9,)), dma((9,)),
             dma((GROUPS,)), dma((GROUPS,)),
@@ -352,7 +376,7 @@
         jnp.transpose(wavefunction, (1, 0, 2)),
         jnp.transpose(left_ops, (1, 0, 2)),
         right_ops.reshape(terms, mr, mr),
-        shifts,
+        term_shift,
     )
     return jnp.transpose(result, (1, 0, 2))
 

time: 82.7 us -> 68.9 us (0.83); the launches traced: 81.1 us -> 68.6 us
  Pallas kernels: 77.8 us -> 66.5 us
  local copies, waits for them, and re-layouts: 3.31 us -> 2.06 us
    pallas_call x1, Pallas kernels: 77.8 us -> 66.5 us  [on_device(): pl.pallas_call(kernel, out_shape=jax.ShapeDtypeStruct((vecs, ml, OWN * mr...]
    pad x1 -> x0, local copies, waits for them, and re-layouts: 1.25 us -> none  [on_device(): shifts = jnp.pad(term_shift.reshape(1, terms), ((0, 7), (0, 128 - terms)))]
where the time goes in v2:
time: 68.9 us; the launch traced here: 68.6 us
  Pallas kernels  66.5 us (97%)
  local copies, waits for them, and re-layouts  2.06 us (3%)
    pallas_call x1, Pallas kernels, on_device(): pl.pallas_call(kernel, out_shape=jax.ShapeDtypeStruct((vecs, ml, OWN * mr...  66.5 us
    unnamed x1, local copies, waits for them, and re-layouts  2.06 us

profile of v2, /device:TPU:16, one launch (start us, length us, event | category | flops | bytes accessed | tf_op | source)
XLA Modules:
  0.0 68.6 jit_solution(9157993715204672458)
XLA Ops:
  0.0 66.5 %shard_map.46 = bf16[3,256,512]{2,1,0:T(8,128)(2,1)} custom-call(bf16[3,256,4096]{2,1,0:T(8,128)(2,1)} %bitcast.5, bf16[3,256,256]{2,1,0:T(8,128)(2,1)} %bitcast.6, bf16[3,128,128]{2,1,0:T(8,128)(2,1)} %bitcast.7, s32[3]{0:T(128)} %sh_in.1), custom_call_target="tpu_custom_call" | custom-call | flops 7247757312 | bytes 4194304 | tf_op jit(solution)/shard_map/pallas_call | solution.py:347
  66.5 2.1 %copy.6 = bf16[256,3,512]{2,0,1:T(8,128)(2,1)} copy(bf16[256,3,512]{2,0,1:T(8,128)(2,1)} %bitcast.4) | data formatting | bytes 1572864

commit v3 on v2

--- a/solution.py
+++ b/solution.py
@@ -1,5 +1,3 @@
-import functools
-
 import jax
 import jax.numpy as jnp
 from jax import lax
@@ -11,12 +9,13 @@
 GROUPS = X * CORES
 SECTORS = Y * Z
 OWN = SECTORS // GROUPS
+EVEN = 1
 MESH = pl.DeviceIdType.MESH
 
 
 def kernel(
     w_hbm, l_hbm, r_hbm, sh_in, out,
-    w, l, r, z, rm, acc, sbuf, rbuf, shv, shs,
+    w, l, r, z, rs, near, acc, sbuf, rbuf, shv, shs,
     loc, ps, pr, zs, zr, ys, yr, ls, lr, ss, sr, os_, or_,
 ):
     op, sec = lax.axis_index("op"), lax.axis_index("sec")
@@ -98,6 +97,10 @@
     def _():
         pl.semaphore_wait(barrier, len(greet))
 
+    turn = 1 - 2 * lax.rem(zz, 2)
+    s0 = lax.div(zz, CORES)
+    order = [s0, lax.rem(s0 - turn + OWN, OWN), lax.rem(s0 + turn + OWN, OWN), lax.rem(s0 + 2, OWN)]
+
     sent = []
 
     def copy(src, dst, send, recv, who):
@@ -124,20 +127,49 @@
 
     for d in range(1, GROUPS):
         push(shv.at[op], shv.at[op], ss.at[d], sr.at[op], (lax.rem(op + d, GROUPS), sec))
-    push(l_hbm, l.at[op], ls.at[2], lr.at[2], sib)
-    push(l_hbm, l.at[op], ls.at[0], lr.at[0], x_up)
-    push(l_hbm, l.at[op], ls.at[1], lr.at[1], x_dn)
+    for i in range(terms):
+        push(l_hbm.at[i], l.at[op, i], ls.at[0, i], lr.at[0, i], x_up)
+        push(l_hbm.at[i], l.at[op, i], ls.at[1, i], lr.at[1, i], x_dn)
+        push(l_hbm.at[i], l.at[op, i], ls.at[2, i], lr.at[2, i], sib)
+    g_dn, g_up, g_far = group(-1), group(1), group(2)
+
+    def left_near(i):
+        blk, part = l.at[g_dn, i], l.at[g_dn, i, :half]
+        got(blk, ls.at[0, i], lr.at[0, i], x_dn)
+        push(part, part, ls.at[5, i], lr.at[5, i], x_up)
+        push(blk, blk, ls.at[3, i], lr.at[3, i], sib)
+        blk, part = l.at[g_up, i], l.at[g_up, i, half:]
+        got(blk, ls.at[1, i], lr.at[1, i], x_up)
+        push(part, part, ls.at[6, i], lr.at[6, i], x_dn)
+        push(blk, blk, ls.at[4, i], lr.at[4, i], sib)
+
+    def left_far(i):
+        part = l.at[g_far, i, :half]
+        got(part, ls.at[5, i], lr.at[5, i], x_dn)
+        push(part, part, ls.at[7, i], lr.at[7, i], sib)
+        part = l.at[g_far, i, half:]
+        got(part, ls.at[6, i], lr.at[6, i], x_up)
+        push(part, part, ls.at[8, i], lr.at[8, i], sib)
+
+    def left_sibling(dx, *ways):
+        for i in range(terms):
+            for way in ways:
+                blk = l.at[group(dx, 1), i]
+                if len(ways) > 1:
+                    blk = l.at[group(dx, 1), i, :half] if way == ways[0] else l.at[group(dx, 1), i, half:]
+                got(blk, ls.at[way, i], lr.at[way, i], sib)
 
     def row_send(c):
         blk = r.at[yy, c]
         push(blk, blk, ys.at[0, c], yr.at[0, c], y_up)
         push(blk, blk, ys.at[1, c], yr.at[1, c], y_dn)
 
-    def passage(c):
+    def passage(c, p):
+        late = sum((p == order[k]).astype(jnp.int32) for k in range(EVEN, OWN)) > 0
         if c:
-            upward = jnp.where(zz == Z - 1, 1, 0)
+            upward = jnp.where((zz == Z - 1) & late, 1, 0)
         else:
-            upward = jnp.where(zz == 0, 0, 1)
+            upward = jnp.where((zz == 0) & late, 0, 1)
         to = (op, y_of(2 * upward - 1) * Z + zz)
         source = (op, y_of(1 - 2 * upward) * Z + zz)
         return 1 - upward, to, source
@@ -145,16 +177,21 @@
     def row_forward(p):
         for c in range(CORES):
             at = p * CORES + c
-            way, to, source = passage(c)
+            way, to, source = passage(c, p)
             blk = r.at[y_of(2 * way - 1), at]
             got(blk, ys.at[way, at], yr.at[way, at], source)
             push(blk, blk, ys.at[2, at], yr.at[2, at], to)
 
-    def row_finish(p):
+    def row_near(p):
         for c in range(CORES):
             at = p * CORES + c
-            way, to, source = passage(c)
+            way, to, _ = passage(c, p)
             got(r.at[y_of(1 - 2 * way), at], ys.at[1 - way, at], yr.at[1 - way, at], to)
+
+    def row_far(p):
+        for c in range(CORES):
+            at = p * CORES + c
+            _, _, source = passage(c, p)
             got(r.at[y_of(2), at], ys.at[2, at], yr.at[2, at], source)
 
     def hop_up(k, i):
@@ -189,20 +226,44 @@
 
         lax.fori_loop(0, terms, one, 0)
 
-    def right_products(p):
-        sigma = sector_of(p)
-        for g in range(GROUPS):
-            for i in range(terms):
-                s = shs[g, 0, i]
-                blk = r[(g // CORES + 2) % Y, p * CORES + g % CORES, i]
-                for q in range(3):
-                    kept = jnp.where(jnp.full(blk.shape, s, jnp.int32) == q - 1, blk, jnp.zeros_like(blk))
-                    rm[g * terms + i, :, q * mr : (q + 1) * mr] = kept
+    per_row = CORES * terms
+
+    def first_term(d):
+        return far_y(y_of(d)) * per_row
+
+    nothing = Y * per_row
+    rs[nothing] = jnp.zeros(rs.shape[1:], rs.dtype)
+
+    def right_blocks(p, rows):
+        for d in rows:
+            for c in range(CORES):
+                for i in range(terms):
+                    rs[(d % Y) * per_row + c * terms + i] = r[y_of(d), p * CORES + c, i]
+
+    def right_of(rows):
+        tall = []
+        for d in rows:
+            for c in range(CORES):
+                for i in range(terms):
+                    s, n = shs[far_y(y_of(d)) * CORES + c, 0, i], (d % Y) * per_row + c * terms + i
+                    tall.append(jnp.concatenate([rs[jnp.where(s == q - 1, n, nothing)] for q in range(3)], axis=1))
+        return jnp.concatenate(tall, axis=0)
+
+    def left_of(sigma, v, rows):
+        return jnp.concatenate([z[sigma, v, first_term(d) + k] for d in rows for k in range(per_row)], axis=1)
+
+    def right_near(p):
+        rows = (0, 1, -1)
+        right_blocks(p, rows)
+        lhs = jnp.concatenate([left_of(sector_of(p), v, rows) for v in range(vecs)], axis=0)
+        near[...] = jnp.dot(lhs, right_of(rows), preferred_element_type=jnp.float32).reshape(near.shape)
+
+    def right_far(p):
+        sigma, rows = sector_of(p), (2,)
+        right_blocks(p, rows)
 
         def one(v, carry):
-            lhs = jnp.concatenate([z[sigma, v, t] for t in range(GROUPS * terms)], axis=1)
-            rhs = rm[...].reshape(GROUPS * terms * mr, 3 * mr)
-            sums = jnp.dot(lhs, rhs, preferred_element_type=jnp.float32)
+            sums = near[v] + jnp.dot(left_of(sigma, v, rows), right_of(rows), preferred_element_type=jnp.float32)
             sbuf[0, sigma, v] = sums[:, :mr].astype(sbuf.dtype)
             acc[sigma, v] = sums[:, mr : 2 * mr]
             sbuf[1, sigma, v] = sums[:, 2 * mr :].astype(sbuf.dtype)
@@ -224,10 +285,6 @@
         hop_up(0, i)
         hop_dn(0, i)
     row_send(zz)
-
-    turn = 1 - 2 * lax.rem(zz, 2)
-    s0 = lax.div(zz, CORES)
-    order = [s0, lax.rem(s0 - turn + OWN, OWN), lax.rem(s0 + turn + OWN, OWN), lax.rem(s0 + 2, OWN)]
 
     for d in range(1, GROUPS):
         g = lax.rem(op + d, GROUPS)
@@ -246,60 +303,60 @@
             pl.when(op < GROUPS - 1)(arrived)
         else:
             arrived()
+    left_near(0)
     left_products(op)
+    left_near(1)
 
     hop(1)
     row_send(z_of(turn))
-
-    got(l.at[group(0, 1)], ls.at[2], lr.at[2], sib)
+    left_sibling(0, 2)
     left_products(group(0, 1))
-
-    g_dn, g_up, g_far = group(-1), group(1), group(2)
-    got(l.at[g_dn], ls.at[0], lr.at[0], x_dn)
-    push(l.at[g_dn, :, :half], l.at[g_dn, :, :half], ls.at[5], lr.at[5], x_up)
-    push(l.at[g_dn], l.at[g_dn], ls.at[3], lr.at[3], sib)
-    got(l.at[g_up], ls.at[1], lr.at[1], x_up)
-    push(l.at[g_up, :, half:], l.at[g_up, :, half:], ls.at[6], lr.at[6], x_dn)
-    push(l.at[g_up], l.at[g_up], ls.at[4], lr.at[4], sib)
+    left_near(2)
 
     hop(2)
     row_send(order[1] * CORES)
     row_send(order[1] * CORES + 1)
+    left_products(g_dn)
     row_forward(order[0])
-
-    left_products(g_dn)
+    left_far(0)
     left_products(g_up)
+    left_far(1)
 
     hop(3)
     row_send(order[2] * CORES)
     row_send(order[2] * CORES + 1)
+    left_far(2)
+    left_sibling(-1, 3)
+    left_products(group(-1, 1))
+    left_sibling(1, 4)
+    left_products(group(1, 1))
     row_forward(order[1])
-
-    got(l.at[g_far, :, :half], ls.at[5], lr.at[5], x_dn)
-    push(l.at[g_far, :, :half], l.at[g_far, :, :half], ls.at[7], lr.at[7], sib)
-    got(l.at[g_far, :, half:], ls.at[6], lr.at[6], x_up)
-    push(l.at[g_far, :, half:], l.at[g_far, :, half:], ls.at[8], lr.at[8], sib)
-    got(l.at[group(-1, 1)], ls.at[3], lr.at[3], sib)
-    left_products(group(-1, 1))
-    got(l.at[group(1, 1)], ls.at[4], lr.at[4], sib)
-    left_products(group(1, 1))
 
     hop(4)
     row_send(order[3] * CORES)
     row_send(order[3] * CORES + 1)
+    left_products(g_far)
+    left_sibling(2, 7, 8)
+    left_products(group(2, 1))
+
+    row_near(order[0])
+    right_near(order[0])
     row_forward(order[2])
-
-    left_products(g_far)
-    got(l.at[group(2, 1), :, :half], ls.at[7], lr.at[7], sib)
-    got(l.at[group(2, 1), :, half:], ls.at[8], lr.at[8], sib)
-    left_products(group(2, 1))
-
-    row_finish(order[0])
-    right_products(order[0])
+    row_far(order[0])
+    right_far(order[0])
+    row_near(order[1])
+    right_near(order[1])
+    row_far(order[1])
+    right_far(order[1])
     row_forward(order[3])
-    for p in order[1:]:
-        row_finish(p)
-        right_products(p)
+    row_near(order[2])
+    right_near(order[2])
+    row_far(order[2])
+    right_far(order[2])
+    row_near(order[3])
+    right_near(order[3])
+    row_far(order[3])
+    right_far(order[3])
 
     def total(sigma, carry):
         for v in range(vecs):
@@ -354,7 +411,8 @@
             pltpu.VMEM((GROUPS, terms, ml, ml), bf16),
             pltpu.VMEM((Y, Z, terms, mr, mr), bf16),
             pltpu.VMEM((OWN, vecs, every, ml, mr), bf16),
-            pltpu.VMEM((every, mr, 3 * mr), bf16),
+            pltpu.VMEM((every + 1, mr, mr), bf16),
+            pltpu.VMEM((vecs, ml, 3 * mr), jnp.float32),
             pltpu.VMEM((OWN, vecs, ml, mr), jnp.float32),
             pltpu.VMEM((2, OWN, vecs, ml, mr), bf16),
             pltpu.VMEM((2, OWN, vecs, ml, mr), bf16),
@@ -364,7 +422,7 @@
             dma((terms,)), dma((terms,)),
             dma((7, terms)), dma((7, terms)),
             dma((3, Z)), dma((3, Z)),
-            dma((9,)), dma((9,)),
+            dma((9, terms)), dma((9, terms)),
             dma((GROUPS,)), dma((GROUPS,)),
             dma((2, OWN, vecs)), dma((2, OWN, vecs)),
         ],

time: 68.9 us -> 66.1 us (0.959)
  Pallas kernels: 66.5 us -> 63.9 us
    pallas_call x1, Pallas kernels: 66.5 us -> 63.9 us  [on_device(): pl.pallas_call(kernel, out_shape=jax.ShapeDtypeStruct((vecs, ml, OWN * mr...]
where the time goes in v3:
time: 66.1 us; the launch traced here: 66 us
  Pallas kernels  63.9 us (97%)
  local copies, waits for them, and re-layouts  2.06 us (3%)
    pallas_call x1, Pallas kernels, on_device(): pl.pallas_call(kernel, out_shape=jax.ShapeDtypeStruct((vecs, ml, OWN * mr...  63.9 us
    unnamed x1, local copies, waits for them, and re-layouts  2.06 us

profile of v3, /device:TPU:16, one launch (start us, length us, event | category | flops | bytes accessed | tf_op | source)
XLA Modules:
  0.0 66.0 jit_solution(9217845552163542100)
XLA Ops:
  0.0 63.9 %shard_map.46 = bf16[3,256,512]{2,1,0:T(8,128)(2,1)} custom-call(bf16[3,256,4096]{2,1,0:T(8,128)(2,1)} %bitcast.5, bf16[3,256,256]{2,1,0:T(8,128)(2,1)} %bitcast.6, bf16[3,128,128]{2,1,0:T(8,128)(2,1)} %bitcast.7, s32[3]{0:T(128)} %sh_in.1), custom_call_target="tpu_custom_call" | custom-call | flops 7247757312 | bytes 4194304 | tf_op jit(solution)/shard_map/pallas_call | solution.py:404
  63.9 2.1 %copy.6 = bf16[256,3,512]{2,0,1:T(8,128)(2,1)} copy(bf16[256,3,512]{2,0,1:T(8,128)(2,1)} %bitcast.4) | data formatting | bytes 1572864

commit v4 on v3

--- a/solution.py
+++ b/solution.py
@@ -81,6 +81,11 @@
         own_shifts = jnp.where(lane == i, jnp.full(lane.shape, sh_in[i], jnp.int32), own_shifts)
     shv[op] = own_shifts
 
+    for q, end in ((0, SECTORS - 1), (1, 0)):
+        @pl.when(sec == end)
+        def _(q=q):
+            rbuf[q] = jnp.zeros(rbuf.shape[1:], rbuf.dtype)
+
     barrier = pltpu.get_barrier_semaphore()
     greet = [z_up, z_dn, y_up, y_dn, s_up, s_dn]
     greet += [(lax.rem(op + d, GROUPS), sec) for d in range(1, GROUPS)]
@@ -226,6 +231,13 @@
 
         lax.fori_loop(0, terms, one, 0)
 
+    has = (sec > 0, sec < SECTORS - 1)
+
+    def shift_copy(q, sigma, v):
+        return copy(
+            sbuf.at[q, sigma, v], rbuf.at[q, sigma, v], os_.at[q, sigma, v], or_.at[q, sigma, v], (s_dn, s_up)[q]
+        )
+
     per_row = CORES * terms
 
     def first_term(d):
@@ -267,8 +279,8 @@
             sbuf[0, sigma, v] = sums[:, :mr].astype(sbuf.dtype)
             acc[sigma, v] = sums[:, mr : 2 * mr]
             sbuf[1, sigma, v] = sums[:, 2 * mr :].astype(sbuf.dtype)
-            for q, who in ((0, s_dn), (1, s_up)):
-                copy(sbuf.at[q, sigma, v], rbuf.at[q, sigma, v], os_.at[q, sigma, v], or_.at[q, sigma, v], who).start()
+            for q in range(2):
+                pl.when(has[q])(lambda q=q: shift_copy(q, sigma, v).start())
             return carry
 
         lax.fori_loop(0, vecs, one, 0)
@@ -358,39 +370,36 @@
     row_far(order[3])
     right_far(order[3])
 
+    for c in sent:
+        c.wait_send()
+
+    @pl.when(moves)
+    def _():
+        for i in range(terms):
+            copy(r_hbm.at[i], r.at[to_y, to_z, i], ps.at[i], pr.at[i], (to_op, to_sec)).wait_send()
+
+    def drain(sigma, carry):
+        for v in range(vecs):
+            for q in range(2):
+                pl.when(has[q])(lambda q=q, v=v: shift_copy(q, sigma, v).wait_send())
+        return carry
+
+    for p in order[:3]:
+        drain(sector_of(p), 0)
+
     def total(sigma, carry):
         for v in range(vecs):
-            got(rbuf.at[0, sigma, v], os_.at[0, sigma, v], or_.at[0, sigma, v], s_up)
-            got(rbuf.at[1, sigma, v], os_.at[1, sigma, v], or_.at[1, sigma, v], s_dn)
+            for q in range(2):
+                pl.when(has[1 - q])(lambda q=q, v=v: shift_copy(q, sigma, v).wait_recv())
         for v in range(vecs):
-            above = rbuf[0, sigma, v].astype(jnp.float32)
-            below = rbuf[1, sigma, v].astype(jnp.float32)
-            whole = acc[sigma, v]
-            whole = whole + jnp.where(jnp.full(above.shape, sec, jnp.int32) < SECTORS - 1, above, 0.0)
-            whole = whole + jnp.where(jnp.full(below.shape, sec, jnp.int32) > 0, below, 0.0)
+            whole = acc[sigma, v] + rbuf[0, sigma, v].astype(jnp.float32) + rbuf[1, sigma, v].astype(jnp.float32)
             at = pl.multiple_of(sigma * mr, mr)
             out[v, :, pl.ds(at, mr)] = whole.astype(out.dtype)
         return carry
 
     lax.fori_loop(0, OWN, total, 0)
 
-    for c in sent:
-        c.wait_send()
-
-    @pl.when(moves)
-    def _():
-        for i in range(terms):
-            copy(r_hbm.at[i], r.at[to_y, to_z, i], ps.at[i], pr.at[i], (to_op, to_sec)).wait_send()
-
-    def drain(sigma, carry):
-        for v in range(vecs):
-            for q, who in ((0, s_dn), (1, s_up)):
-                copy(
-                    sbuf.at[q, sigma, v], rbuf.at[q, sigma, v], os_.at[q, sigma, v], or_.at[q, sigma, v], who
-                ).wait_send()
-        return carry
-
-    lax.fori_loop(0, OWN, drain, 0)
+    drain(sector_of(order[3]), 0)
 
 
 def on_device(wavefunction, left_ops, right_ops, term_shift):

time: 66.1 us -> 66 us (level)
  no operation moved by 1% of the time
where the time goes in v4:
time: 66 us; the launch traced here: 65.9 us
  Pallas kernels  63.8 us (97%)
  local copies, waits for them, and re-layouts  2.06 us (3%)
    pallas_call x1, Pallas kernels, on_device(): pl.pallas_call(kernel, out_shape=jax.ShapeDtypeStruct((vecs, ml, OWN * mr...  63.8 us
    unnamed x1, local copies, waits for them, and re-layouts  2.06 us

profile of v4, /device:TPU:16, one launch (start us, length us, event | category | flops | bytes accessed | tf_op | source)
XLA Modules:
  0.0 65.9 jit_solution(16182453462504311573)
XLA Ops:
  0.0 63.8 %shard_map.46 = bf16[3,256,512]{2,1,0:T(8,128)(2,1)} custom-call(bf16[3,256,4096]{2,1,0:T(8,128)(2,1)} %bitcast.5, bf16[3,256,256]{2,1,0:T(8,128)(2,1)} %bitcast.6, bf16[3,128,128]{2,1,0:T(8,128)(2,1)} %bitcast.7, s32[3]{0:T(128)} %sh_in.1), custom_call_target="tpu_custom_call" | custom-call | flops 7247757312 | bytes 4194304 | tf_op jit(solution)/shard_map/pallas_call | solution.py:413
  63.8 2.1 %copy.6 = bf16[256,3,512]{2,0,1:T(8,128)(2,1)} copy(bf16[256,3,512]{2,0,1:T(8,128)(2,1)} %bitcast.4) | data formatting | bytes 1572864
